TPU v7x, 128 devices: a whole 4x4x4 slice. The times are simulated.
128 devices in a mesh: row: 8 (over x, y_hi), col: 16 (over y_lo, z, core).
Axes of the slice: x: 4, y: 4 (y_hi: 2, y_lo: 2; y = y_hi * 2 + y_lo), z: 4, core: 2. Of those that a mesh axis runs over, the one named last changes fastest.
Arguments:
- train_inputs: bfloat16 [512, 8192], P(('row', 'col')), may hold values from -6 to 6
- train_grads: bfloat16 [512, 8192], P(('row', 'col')), may hold values from -6 to 6
- query_inputs: bfloat16 [256, 8192], P(('row', 'col')), may hold values from -6 to 6
- query_grads: bfloat16 [256, 8192], P(('row', 'col')), may hold values from -6 to 6
- input_basis: bfloat16 [8192, 8192], P('row', 'col'), may hold values from -0.0625 to 0.0625
- output_basis: bfloat16 [8192, 8192], P('col', 'row'), may hold values from -0.0625 to 0.0625
- eigenvalues: float32 [8192, 8192], P('row', 'col'), may hold values from 0.5 to 5
- query_starts: int32 [16], replicated, may hold values from 0 to 255, as said below
- query_ends: int32 [16], replicated, may hold values from 1 to 256, as said below
Outputs:
- scores: float32 [16, 512], replicated
Inputs may be any that keep to these rules, and one draw needn't show every extreme that they name: Query q covers the query rows query_starts[q] <= r < query_ends[q]: a nonempty span of at most 128 rows that lies inside one aligned block of 128 rows (rows k * 128 to (k + 1) * 128 - 1); spans of different queries may intersect or share a block. `query_ends`: see query_starts.
All inputs are finite; a program needn't handle non-finite values.
Results may differ from a plain program's by a relative error of at most 0.005.
Values may be sent and summed in bfloat16 or wider, within the bound.
A program may use at most 64 MiB of HBM per device.

v0:
```python
import math
import jax
import jax.numpy as jnp
from jax import lax
from jax.sharding import Mesh
from jax.sharding import PartitionSpec as P

D_IN = 8192
D_OUT = 8192
QBLOCK = 128
COL = ("col_0", "col_1", "col_2")
ROW = ("row_0", "row_1")
ROW_COL = ("row_0", "row_1", "col_0", "col_1", "col_2")
damping = 0.1


def laid_out(parts, dim):
    parts = jnp.moveaxis(parts, 0, dim)
    dims = parts.shape
    return parts.reshape(*dims[:dim], dims[dim] * dims[dim + 1], *dims[dim + 2 :])


def gather_together(arrays, axis, dims):
    line = jnp.concatenate([a.reshape(-1) for a in arrays])
    lines, at, gathered = (lax.all_gather(line, axis), 0, [])
    for a, dim in zip(arrays, dims):
        parts = lines[:, at : at + a.size].reshape(-1, *a.shape)
        gathered.append(laid_out(parts, dim))
        at += a.size
    return tuple(gathered)


def by_axis(value, axes):
    for axis in axes:
        value = lax.psum(value, axis)
    return value


def shards(
    train_inputs,
    train_grads,
    query_inputs,
    query_grads,
    input_basis,
    output_basis,
    eigenvalues,
    query_starts,
    query_ends,
):
    grouped = gather_together((train_inputs, query_inputs), COL, (0, 0))
    train_in, query_in = (
        lax.all_to_all(grouped[0], ROW, split_axis=1, concat_axis=0, tiled=True),
        lax.all_to_all(grouped[1], ROW, split_axis=1, concat_axis=0, tiled=True),
    )
    spread = (
        lax.all_to_all(train_grads, COL, split_axis=1, concat_axis=0, tiled=True),
        lax.all_to_all(query_grads, COL, split_axis=1, concat_axis=0, tiled=True),
    )
    train_out, query_out = gather_together((spread[0], spread[1]), ROW, (0, 0))
    train_in_part = jnp.dot(train_in, input_basis, preferred_element_type=jnp.float32)
    query_in_part = jnp.dot(query_in, input_basis, preferred_element_type=jnp.float32)
    train_out_part = jnp.dot(train_out, output_basis, preferred_element_type=jnp.float32)
    query_out_part = jnp.dot(query_out, output_basis, preferred_element_type=jnp.float32)
    in_sums = lax.psum((train_in_part, query_in_part), ROW)
    out_sums = lax.psum((train_out_part, query_out_part), COL)
    train_in_rot = in_sums[0].astype(jnp.bfloat16)
    query_in_rot = in_sums[1].astype(jnp.bfloat16)
    train_grad_rot = out_sums[0].astype(jnp.bfloat16)
    query_grad_rot = out_sums[1].astype(jnp.bfloat16)
    grads_wide = train_grad_rot.astype(jnp.float32)
    denominator = eigenvalues + damping

    def per_query(span):
        span_start, span_end = span
        block_top = span_start // QBLOCK * QBLOCK
        grad_rows = lax.dynamic_slice_in_dim(query_grad_rot, block_top, QBLOCK, 0)
        input_rows = lax.dynamic_slice_in_dim(query_in_rot, block_top, QBLOCK, 0)
        positions = block_top + jnp.arange(QBLOCK, dtype=jnp.int32)
        inside = (positions >= span_start) & (positions < span_end)
        grad_rows = jnp.where(inside[:, None], grad_rows, jnp.zeros((), grad_rows.dtype))
        outer_sum = lax.dot_general(
            grad_rows, input_rows, (((0,), (0,)), ((), ())), preferred_element_type=jnp.float32
        )
        scaled = (outer_sum / denominator).astype(jnp.bfloat16)
        paired = lax.dot_general(
            train_in_rot, scaled, (((1,), (1,)), ((), ())), preferred_element_type=jnp.float32
        )
        return jnp.sum(grads_wide * paired, axis=1)

    partial_scores = lax.map(per_query, (query_starts, query_ends))
    totals = by_axis(partial_scores, ROW_COL)
    return totals * (1.0 / math.sqrt(D_IN * D_OUT * QBLOCK))


def solution(mesh):
    split = Mesh(mesh.devices.reshape(4, 2, 2, 4, 2), ("row_0", "row_1", "col_0", "col_1", "col_2"))
    placed = (
        P(ROW_COL, None),
        P(ROW_COL, None),
        P(ROW_COL, None),
        P(ROW_COL, None),
        P(ROW, COL),
        P(COL, ROW),
        P(ROW, COL),
        P(),
        P(),
    )
    return jax.shard_map(shards, mesh=split, in_specs=placed, out_specs=P(), check_vma=False)
```

profile of v0, /device:TPU:1, one launch (start us, length us, event | category | flops | bytes accessed | tf_op | source)
XLA Modules:
  0.0 458.6 jit_solution(13673715249605043826)
XLA Ops:
  6.5 0.9 copy.26
  7.5 0.8 copy.27
  8.2 0.6 pad_maximum_fusion.1
  8.9 13.6 %all_to_all.70 = bf16[2,16,512]{2,0,1:T(2,128)(2,1)S(1)} all-to-all(bf16[2,16,512]{2,0,1:T(2,128)(2,1)} %bitcast.54), channel_id=1, replica_groups=mesh['row_0'=4,'row_1'=2,'col_0'=2,'col_1'=4,'col_2'=2] {'col_0','col_1'..., dimensions={1} | all-to-all | bytes 65536 | tf_op jit(solution)/shard_map/all_to_all | solution.py:57
  22.6 3.7 all-to-all-start
  26.2 3.2 broadcast_add_fusion
  29.5 2.7 all-to-all-done
  32.2 31.4 %all-gather = bf16[393216]{0:T(1024)(128)(2,1)S(1)} all-gather(bf16[49152]{0:T(1024)(128)(2,1)S(1)} %pad_maximum_fusion), channel_id=2, replica_groups=mesh['row_0'=4,'row_1'=2,'col_0'=2,'col_1'=4,'col_2'=2] {'row_0','row_1'}, dimensions={0}, use_global_device_ids=true | all-gather | bytes 884736 | tf_op jit(solution)/shard_map/all_gather | solution.py:25
  64.0 1.0 reshape_reshape.9
  65.0 1.8 reshape.40
  66.9 0.9 slice.17
  67.7 1.3 all_to_all.58
  69.0 1.1 copy.21
  70.1 4.5 all-to-all-start.2
  74.7 1.8 fusion.18
  76.4 0.8 reshape_reshape.8
  77.3 2.5 fusion.15
  79.7 1.1 slice.18
  80.8 2.3 all_to_all.62
  83.1 2.8 copy.22
  85.9 6.6 %all-to-all-start.3 = ((bf16[64,8,1024]{2,0,1:T(8,128)(2,1)}), bf16[64,8,1024]{2,0,1:T(8,128)(2,1)}, u32[]{:S(2)}, u32[]{:S(2)}) async-start(bf16[64,8,1024]{2,0,1:T(8,128)(2,1)} %copy.22), calls=%async_computation.3 | async-start | bytes 2097152 | tf_op jit(solution)/shard_map/all_to_all | solution.py:52
  92.6 74.4 %all-reduce.4 = (bf16[256,1024]{1,0:T(8,128)(2,1)}, bf16[512,1024]{1,0:T(8,128)(2,1)}) all-reduce(f32[256,1024]{1,0:T(8,128)} %fusion.15, f32[512,1024]{1,0:T(8,128)S(1)} %fusion.18), channel_id=1, replica_groups=mesh['row_0'=4,'row_1'=2,'col_0'=2,'col_1'=4,'col_2'=2] {'col_0','col_1'..., use_global_device_ids=true, to_apply=%region_0.0 | all-reduce | flops 786432 | bytes 4718592 | tf_op jit(solution)/shard_map/psum | solution.py:65
  166.9 1.5 copy.23
  168.4 2.6 fusion.16
  171.0 3.3 fusion.17
  174.3 81.4 %all-reduce.5 = (bf16[256,512]{1,0:T(8,128)(2,1)}, bf16[512,512]{1,0:T(8,128)(2,1)}) all-reduce(f32[256,512]{1,0:T(8,128)} %fusion.16, f32[512,512]{1,0:T(8,128)} %fusion.17), channel_id=1, replica_groups=mesh['row_0'=4,'row_1'=2,'col_0'=2,'col_1'=4,'col_2'=2] {'row_0','row_1'}, use_global_device_ids=true, to_apply=%region_1.0 | all-reduce | flops 393216 | bytes 2359296 | tf_op jit(solution)/shard_map/psum | solution.py:64
  255.7 127.2 %while.12 = (s32[]{:T(128)}, f32[16,512]{1,0:T(8,128)S(1)}, s32[16]{0:T(128)S(1)}, s32[16]{0:T(128)S(1)}, bf16[256,1024]{1,0:T(8,128)(2,1)}, /*index=5*/bf16[256...) while((s32[]{:T(128)}, f32[16,512]{1,0:T(8,128)S(1)}, ...), condition=%wide.region_6.7_spmd, body=%wide.region_4.6_spmd.sunk | while | flops 673316864 | bytes 5119617 | solution.py:90
  259.4 1.2 compare_and_fusion.2
  260.6 2.9 fusion.35
  267.4 1.2 compare_and_fusion.2
  268.6 2.9 fusion.35
  275.3 1.2 compare_and_fusion.2
  276.6 2.9 fusion.35
  283.3 1.2 compare_and_fusion.2
  284.5 2.9 fusion.35
  291.2 1.2 compare_and_fusion.2
  292.5 2.9 fusion.35
  299.2 1.2 compare_and_fusion.2
  300.4 2.9 fusion.35
  307.1 1.2 compare_and_fusion.2
  308.4 2.9 fusion.35
  315.1 1.2 compare_and_fusion.2
  316.3 2.9 fusion.35
  323.0 1.2 compare_and_fusion.2
  324.3 2.9 fusion.35
  331.0 1.2 compare_and_fusion.2
  332.2 2.9 fusion.35
  338.9 1.2 compare_and_fusion.2
  340.2 2.9 fusion.35
  346.9 1.2 compare_and_fusion.2
  348.1 2.9 fusion.35
  354.9 1.2 compare_and_fusion.2
  356.1 2.9 fusion.35
  362.8 1.2 compare_and_fusion.2
  364.0 2.9 fusion.35
  370.8 1.2 compare_and_fusion.2
  372.0 2.9 fusion.35
  378.7 1.2 compare_and_fusion.2
  380.0 2.9 fusion.35
  383.0 11.8 %psum.67 = f32[16,512]{1,0:T(8,128)S(1)} all-reduce(f32[16,512]{1,0:T(8,128)S(1)} %get-tuple-element.119), channel_id=1, replica_groups=mesh['row_0'=4,'row_1'=2,'col_0'=2,'col_1'=4,'col_2'=2] {'row_0'}, use_global_device_ids=true, to_apply=%region_7.8 | all-reduce | flops 8192 | bytes 65536 | tf_op jit(solution)/shard_map/psum | solution.py:35
  394.8 7.5 %psum.68 = f32[16,512]{1,0:T(8,128)S(1)} all-reduce(f32[16,512]{1,0:T(8,128)S(1)} %psum.67), channel_id=1, replica_groups=mesh['row_0'=4,'row_1'=2,'col_0'=2,'col_1'=4,'col_2'=2] {'row_1'}, use_global_device_ids=true, to_apply=%region_8.9 | all-reduce | flops 8192 | bytes 65536 | tf_op jit(solution)/shard_map/psum | solution.py:35
  402.3 6.6 %psum.69 = f32[16,512]{1,0:T(8,128)S(1)} all-reduce(f32[16,512]{1,0:T(8,128)S(1)} %psum.68), channel_id=1, replica_groups=mesh['row_0'=4,'row_1'=2,'col_0'=2,'col_1'=4,'col_2'=2] {'col_0'}, use_global_device_ids=true, to_apply=%region_9.10 | all-reduce | flops 8192 | bytes 65536 | tf_op jit(solution)/shard_map/psum | solution.py:35
  409.0 18.8 %psum.70 = f32[16,512]{1,0:T(8,128)S(1)} all-reduce(f32[16,512]{1,0:T(8,128)S(1)} %psum.69), channel_id=1, replica_groups=mesh['row_0'=4,'row_1'=2,'col_0'=2,'col_1'=4,'col_2'=2] {'col_1'}, use_global_device_ids=true, to_apply=%region_10.11 | all-reduce | flops 8192 | bytes 65536 | tf_op jit(solution)/shard_map/psum | solution.py:35
  427.7 23.4 %psum.71 = f32[16,512]{1,0:T(8,128)S(1)} all-reduce(f32[16,512]{1,0:T(8,128)S(1)} %psum.70), channel_id=1, replica_groups=mesh['row_0'=4,'row_1'=2,'col_0'=2,'col_1'=4,'col_2'=2] {'col_2'}, use_global_device_ids=true, to_apply=%region_11.12 | all-reduce | flops 8192 | bytes 65536 | tf_op jit(solution)/shard_map/psum | solution.py:35
  (74 shorter events, 21.5 us)
Async XLA Ops:
  6.5 68.1 %copy-start = (bf16[512,1024]{1,0:T(8,128)(2,1)S(1)}, bf16[512,1024]{1,0:T(8,128)(2,1)}, u32[]{:S(2)}) copy-start(bf16[512,1024]{1,0:T(8,128)(2,1)} %param.16) | copy-start | bytes 3145732
  6.5 58.5 %all-gather.4.cloned.1.call-start = ((), (), s32[]{:S(2)}) async-start(), calls=%async_computation.4 | async-start | bytes 1671168 | tf_op jit(solution)/shard_map/all_gather | solution.py:25
  22.6 9.6 %all-to-all-start = ((bf16[4,16,512]{2,0,1:T(4,128)(2,1)}), bf16[4,16,512]{2,0,1:T(4,128)(2,1)S(1)}, u32[]{:S(2)}, u32[]{:S(2)}) async-start(bf16[4,16,512]{2,0,1:T(4,128)(2,1)} %bitcast.51), calls=%async_computation | async-start | bytes 131072 | tf_op jit(solution)/shard_map/all_to_all | solution.py:56
  63.9 1.1 copy-start.3
  66.8 3.3 copy-start.1
  70.1 6.3 %slice-start = ((bf16[8,49152]{1,0:T(8,128)(2,1)}), bf16[8,16384]{1,0:T(8,128)(2,1)S(1)}, s32[]{:S(2)}) async-start(bf16[8,49152]{1,0:T(8,128)(2,1)} %copy-done.3), calls=%async_computation.5 | async-start | bytes 524288 | tf_op jit(solution)/shard_map/slice | solution.py:27
  70.1 15.8 %all-to-all-start.2 = ((bf16[32,8,1024]{2,0,1:T(8,128)(2,1)}), bf16[32,8,1024]{2,0,1:T(8,128)(2,1)}, u32[]{:S(2)}, u32[]{:S(2)}) async-start(bf16[32,8,1024]{2,0,1:T(8,128)(2,1)} %copy.21), calls=%async_computation.2 | async-start | bytes 1048576 | tf_op jit(solution)/shard_map/all_to_all | solution.py:53
  77.2 2.5 copy-start.2
  85.9 85.1 %all-to-all-start.3 = ((bf16[64,8,1024]{2,0,1:T(8,128)(2,1)}), bf16[64,8,1024]{2,0,1:T(8,128)(2,1)}, u32[]{:S(2)}, u32[]{:S(2)}) async-start(bf16[64,8,1024]{2,0,1:T(8,128)(2,1)} %copy.22), calls=%async_computation.3 | async-start | bytes 2097152 | tf_op jit(solution)/shard_map/all_to_all | solution.py:52
  171.0 84.7 %copy-start.4 = (s32[16]{0:T(128)S(1)}, s32[16]{0:T(128)}, u32[]{:S(2)}) copy-start(s32[16]{0:T(128)} %param.18) | copy-start | bytes 196
  171.0 84.7 %copy-start.5 = (s32[16]{0:T(128)S(1)}, s32[16]{0:T(128)}, u32[]{:S(2)}) copy-start(s32[16]{0:T(128)} %param.19) | copy-start | bytes 196
Sparse Core Ops, SparseCore 0:
  9.1 38.4 all-gather.3
where the time goes:
time: 461 us; the launch traced here: 459 us
  blocking collectives  269 us (58%)
  matrix products  56.8 us (12%)
  loops' own time  40.5 us (9%)
  local copies, waits for them, and re-layouts  37.2 us (8%)
  other arithmetic  24.1 us (5%)
  starting transfers between devices  14.8 us (3%)
  between operations  13.5 us (3%)
    psum x1, blocking collectives, shards(): in_sums = lax.psum((train_in_part, query_in_part), ROW)  81.4 us
    psum x1, blocking collectives, shards(): out_sums = lax.psum((train_out_part, query_out_part), COL)  74.4 us
    psum x5, blocking collectives, by_axis(): value = lax.psum(value, axis)  68.1 us
    dot_general x16, matrix products, per_query(): lax.dot_general(train_in_rot, scaled, (((1,), (1,)), ((), ())), preferred...  46.7 us
    another operation x1, loops' own time, shards(): partial_scores = lax.map(per_query, (query_starts, query_ends))  40.5 us
    all_gather x1, blocking collectives, gather_together(): lines, at, gathered = (lax.all_gather(line, axis), 0, [])  31.4 us
    and x16, other arithmetic, per_query(): inside = (positions >= span_start) & (positions < span_end)  19.6 us
    dynamic_slice x32, local copies, waits for them, and re-layouts, shards(): partial_scores = lax.map(per_query, (query_starts, query_ends))  19.4 us
  transfers between devices with their start and end apart: 4, of which 1 were waited for; matrix products, arithmetic and copies ran while one was open for 4% of the time, Pallas kernels for 0%

commit v1 on v0

--- a/solution.py
+++ b/solution.py
@@ -61,7 +61,7 @@
     query_in_part = jnp.dot(query_in, input_basis, preferred_element_type=jnp.float32)
     train_out_part = jnp.dot(train_out, output_basis, preferred_element_type=jnp.float32)
     query_out_part = jnp.dot(query_out, output_basis, preferred_element_type=jnp.float32)
-    in_sums = lax.psum((train_in_part, query_in_part), ROW)
+    in_sums = lax.psum(lax.psum((train_in_part, query_in_part), "row_1"), "row_0")
     out_sums = lax.psum((train_out_part, query_out_part), COL)
     train_in_rot = in_sums[0].astype(jnp.bfloat16)
     query_in_rot = in_sums[1].astype(jnp.bfloat16)

time: 461 us -> 444 us (0.963)
  blocking collectives: 269 us -> 235 us
  waiting for transfers between devices: 2.68 us -> 23.1 us
    psum x1, blocking collectives: 81.4 us -> 32.8 us  [shards(): lax.psum(lax.psum((train_in_part, query_in_part), 'row_1'), 'row_0')]
    all_gather x1, waiting for transfers between devices: 0.01 us -> 19.8 us  [gather_together(): lines, at, gathered = (lax.all_gather(line, axis), 0, [])]
    psum x1, blocking collectives: 74.4 us -> 92.3 us  [shards(): out_sums = lax.psum((train_out_part, query_out_part), COL)]
    psum x5, blocking collectives: 68.1 us -> 56.5 us  [by_axis(): value = lax.psum(value, axis)]
    all_gather x1, blocking collectives: 31.4 us -> 39.5 us  [gather_together(): lines, at, gathered = (lax.all_gather(line, axis), 0, [])]
  transfers between devices with their start and end apart: 4 -> 5, of which waited for: 1 -> 2; matrix products, arithmetic and copies ran while one was open for 4% -> 5% of each run, Pallas kernels for 0% -> 0%
where the time goes in v1:
time: 444 us; the launch traced here: 442 us
  blocking collectives  235 us (53%)
  matrix products  56.6 us (13%)
  loops' own time  40.5 us (9%)
  local copies, waits for them, and re-layouts  35.1 us (8%)
  other arithmetic  24.1 us (5%)
  waiting for transfers between devices  23.1 us (5%)
  starting transfers between devices  14.1 us (3%)
  between operations  13.6 us (3%)
    psum x1, blocking collectives, shards(): out_sums = lax.psum((train_out_part, query_out_part), COL)  92.3 us
    psum x5, blocking collectives, by_axis(): value = lax.psum(value, axis)  56.5 us
    dot_general x16, matrix products, per_query(): lax.dot_general(train_in_rot, scaled, (((1,), (1,)), ((), ())), preferred...  46.7 us
    another operation x1, loops' own time, shards(): partial_scores = lax.map(per_query, (query_starts, query_ends))  40.5 us
    all_gather x1, blocking collectives, gather_together(): lines, at, gathered = (lax.all_gather(line, axis), 0, [])  39.5 us
    psum x1, blocking collectives, shards(): lax.psum(lax.psum((train_in_part, query_in_part), 'row_1'), 'row_0')  32.8 us
    all_gather x1, waiting for transfers between devices, gather_together(): lines, at, gathered = (lax.all_gather(line, axis), 0, [])  19.8 us
    and x16, other arithmetic, per_query(): inside = (positions >= span_start) & (positions < span_end)  19.6 us
  transfers between devices with their start and end apart: 5, of which 2 were waited for; matrix products, arithmetic and copies ran while one was open for 5% of the time, Pallas kernels for 0%

profile of v1, /device:TPU:1, one launch (start us, length us, event | category | flops | bytes accessed | tf_op | source)
XLA Modules:
  0.0 441.8 jit_solution(4286991284614033062)
XLA Ops:
  6.5 0.9 copy.26
  7.5 0.8 copy.27
  8.9 13.6 %all_to_all.70 = bf16[2,16,512]{2,0,1:T(2,128)(2,1)S(1)} all-to-all(bf16[2,16,512]{2,0,1:T(2,128)(2,1)} %bitcast.55), channel_id=1, replica_groups=mesh['row_0'=4,'row_1'=2,'col_0'=2,'col_1'=4,'col_2'=2] {'col_0','col_1'..., dimensions={1} | all-to-all | bytes 65536 | tf_op jit(solution)/shard_map/all_to_all | solution.py:57
  22.6 3.7 all-to-all-start
  26.2 19.8 %all-gather.4.cloned.1.call-done = bf16[786432]{0:T(1024)(128)(2,1)} async-done(((bf16[49152]{0:T(1024)(128)(2,1)}), bf16[786432]{0:T(1024)(128)(2,1)}) %all-gather.4.cloned.1.call-update) | async-done | bytes 1572880 | tf_op jit(solution)/shard_map/all_gather | solution.py:25
  46.1 1.8 reshape.40
  47.9 0.8 slice.17
  48.7 1.3 all_to_all.58
  50.0 1.1 copy.21
  51.1 6.1 %all-to-all-start.2 = ((bf16[32,8,1024]{2,0,1:T(8,128)(2,1)}), bf16[32,8,1024]{2,0,1:T(8,128)(2,1)S(1)}, u32[]{:S(2)}, u32[]{:S(2)}) async-start(bf16[32,8,1024]{2,0,1:T(8,128)(2,1)} %copy.21), calls=%async_computation.2 | async-start | bytes 1048576 | tf_op jit(solution)/shard_map/all_to_all | solution.py:53
  57.2 3.2 broadcast_add_fusion
  60.5 1.1 slice.18
  61.5 1.6 all_to_all.62
  63.1 1.6 copy.22
  64.6 3.3 all-to-all-done.2
  67.9 4.2 all-to-all-start.3
  72.2 39.5 %all-gather = bf16[393216]{0:T(1024)(128)(2,1)S(1)} all-gather(bf16[49152]{0:T(1024)(128)(2,1)S(1)} %pad_maximum_fusion), channel_id=2, replica_groups=mesh['row_0'=4,'row_1'=2,'col_0'=2,'col_1'=4,'col_2'=2] {'row_0','row_1'}, dimensions={0}, use_global_device_ids=true | all-gather | bytes 884736 | tf_op jit(solution)/shard_map/all_gather | solution.py:25
  112.1 1.0 reshape_reshape.9
  113.2 2.4 fusion.16
  115.6 3.2 fusion.17
  118.9 1.8 fusion.18
  120.7 0.8 reshape_reshape.8
  121.5 2.4 fusion.15
  123.9 92.3 %all-reduce.9 = (bf16[256,1024]{1,0:T(8,128)(2,1)}, bf16[512,1024]{1,0:T(8,128)(2,1)}) all-reduce(f32[256,1024]{1,0:T(8,128)} %fusion.15, f32[512,1024]{1,0:T(8,128)S(1)} %fusion.18), channel_id=1, replica_groups=mesh['row_0'=4,'row_1'=2,'col_0'=2,'col_1'=4,'col_2'=2] {'col_0','col_1'..., use_global_device_ids=true, to_apply=%region_0.0 | all-reduce | flops 786432 | bytes 4718592 | tf_op jit(solution)/shard_map/psum | solution.py:65
  216.2 1.5 copy.23
  217.8 32.8 %all-reduce.8 = (bf16[256,512]{1,0:T(8,128)(2,1)}, bf16[512,512]{1,0:T(8,128)(2,1)}) all-reduce(f32[256,512]{1,0:T(8,128)} %get-tuple-element.178, f32[512,512]{1,0:T(8,128)} %get-tuple-element.179), channel_id=1, replica_groups=mesh['row_0'=4,'row_1'=2,'col_0'=2,'col_1'=4,'col_2'=2] {'row_0'}, use_global_device_ids=true, to_apply=%region_2.0 | all-reduce | flops 393216 | bytes 2359296 | tf_op jit(solution)/shard_map/psum | solution.py:64
  250.6 127.2 %while.12 = (s32[]{:T(128)}, f32[16,512]{1,0:T(8,128)S(1)}, s32[16]{0:T(128)S(1)}, s32[16]{0:T(128)S(1)}, bf16[256,1024]{1,0:T(8,128)(2,1)}, /*index=5*/bf16[256...) while((s32[]{:T(128)}, f32[16,512]{1,0:T(8,128)S(1)}, ...), condition=%wide.region_8.9_spmd, body=%wide.region_6.8_spmd.sunk | while | flops 673316864 | bytes 5119617 | solution.py:90
  254.3 1.2 compare_and_fusion.2
  255.5 2.9 fusion.35
  262.2 1.2 compare_and_fusion.2
  263.5 2.9 fusion.35
  270.2 1.2 compare_and_fusion.2
  271.4 2.9 fusion.35
  278.1 1.2 compare_and_fusion.2
  279.4 2.9 fusion.35
  286.1 1.2 compare_and_fusion.2
  287.3 2.9 fusion.35
  294.0 1.2 compare_and_fusion.2
  295.3 2.9 fusion.35
  302.0 1.2 compare_and_fusion.2
  303.2 2.9 fusion.35
  309.9 1.2 compare_and_fusion.2
  311.2 2.9 fusion.35
  317.9 1.2 compare_and_fusion.2
  319.1 2.9 fusion.35
  325.8 1.2 compare_and_fusion.2
  327.1 2.9 fusion.35
  333.8 1.2 compare_and_fusion.2
  335.0 2.9 fusion.35
  341.8 1.2 compare_and_fusion.2
  343.0 2.9 fusion.35
  349.7 1.2 compare_and_fusion.2
  350.9 2.9 fusion.35
  357.7 1.2 compare_and_fusion.2
  358.9 2.9 fusion.35
  365.6 1.2 compare_and_fusion.2
  366.9 2.9 fusion.35
  373.6 1.2 compare_and_fusion.2
  374.8 2.9 fusion.35
  377.8 11.9 %psum.83 = f32[16,512]{1,0:T(8,128)S(1)} all-reduce(f32[16,512]{1,0:T(8,128)S(1)} %get-tuple-element.119), channel_id=1, replica_groups=mesh['row_0'=4,'row_1'=2,'col_0'=2,'col_1'=4,'col_2'=2] {'row_0'}, use_global_device_ids=true, to_apply=%region_9.10 | all-reduce | flops 8192 | bytes 65536 | tf_op jit(solution)/shard_map/psum | solution.py:35
  389.7 7.3 %psum.84 = f32[16,512]{1,0:T(8,128)S(1)} all-reduce(f32[16,512]{1,0:T(8,128)S(1)} %psum.83), channel_id=1, replica_groups=mesh['row_0'=4,'row_1'=2,'col_0'=2,'col_1'=4,'col_2'=2] {'row_1'}, use_global_device_ids=true, to_apply=%region_10.11 | all-reduce | flops 8192 | bytes 65536 | tf_op jit(solution)/shard_map/psum | solution.py:35
  397.0 6.5 %psum.85 = f32[16,512]{1,0:T(8,128)S(1)} all-reduce(f32[16,512]{1,0:T(8,128)S(1)} %psum.84), channel_id=1, replica_groups=mesh['row_0'=4,'row_1'=2,'col_0'=2,'col_1'=4,'col_2'=2] {'col_0'}, use_global_device_ids=true, to_apply=%region_11.12 | all-reduce | flops 8192 | bytes 65536 | tf_op jit(solution)/shard_map/psum | solution.py:35
  403.5 14.1 %psum.86 = f32[16,512]{1,0:T(8,128)S(1)} all-reduce(f32[16,512]{1,0:T(8,128)S(1)} %psum.85), channel_id=1, replica_groups=mesh['row_0'=4,'row_1'=2,'col_0'=2,'col_1'=4,'col_2'=2] {'col_1'}, use_global_device_ids=true, to_apply=%region_12.13 | all-reduce | flops 8192 | bytes 65536 | tf_op jit(solution)/shard_map/psum | solution.py:35
  417.6 16.8 %psum.87 = f32[16,512]{1,0:T(8,128)S(1)} all-reduce(f32[16,512]{1,0:T(8,128)S(1)} %psum.86), channel_id=1, replica_groups=mesh['row_0'=4,'row_1'=2,'col_0'=2,'col_1'=4,'col_2'=2] {'col_2'}, use_global_device_ids=true, to_apply=%region_13.14 | all-reduce | flops 8192 | bytes 65536 | tf_op jit(solution)/shard_map/psum | solution.py:35
  (73 shorter events, 22.2 us)
Async XLA Ops:
  6.5 112.3 %copy-start = (bf16[512,1024]{1,0:T(8,128)(2,1)S(1)}, bf16[512,1024]{1,0:T(8,128)(2,1)}, u32[]{:S(2)}) copy-start(bf16[512,1024]{1,0:T(8,128)(2,1)} %param.16) | copy-start | bytes 3145732
  6.5 39.5 %all-gather.4.cloned.1.call-start = ((), (), s32[]{:S(2)}) async-start(), calls=%async_computation.4 | async-start | bytes 1671168 | tf_op jit(solution)/shard_map/all_gather | solution.py:25
  22.6 28.5 %all-to-all-start = ((bf16[4,16,512]{2,0,1:T(4,128)(2,1)}), bf16[4,16,512]{2,0,1:T(4,128)(2,1)S(1)}, u32[]{:S(2)}, u32[]{:S(2)}) async-start(bf16[4,16,512]{2,0,1:T(4,128)(2,1)} %bitcast.52), calls=%async_computation | async-start | bytes 131072 | tf_op jit(solution)/shard_map/all_to_all | solution.py:56
  51.1 16.8 %all-to-all-start.2 = ((bf16[32,8,1024]{2,0,1:T(8,128)(2,1)}), bf16[32,8,1024]{2,0,1:T(8,128)(2,1)S(1)}, u32[]{:S(2)}, u32[]{:S(2)}) async-start(bf16[32,8,1024]{2,0,1:T(8,128)(2,1)} %copy.21), calls=%async_computation.2 | async-start | bytes 1048576 | tf_op jit(solution)/shard_map/all_to_all | solution.py:53
  67.9 47.7 %all-to-all-start.3 = ((bf16[64,8,1024]{2,0,1:T(8,128)(2,1)}), bf16[64,8,1024]{2,0,1:T(8,128)(2,1)}, u32[]{:S(2)}, u32[]{:S(2)}) async-start(bf16[64,8,1024]{2,0,1:T(8,128)(2,1)} %copy.22), calls=%async_computation.3 | async-start | bytes 2097152 | tf_op jit(solution)/shard_map/all_to_all | solution.py:52
  72.1 145.6 %all-reduce.7.cloned.1.call-start = ((), (), s32[]{:S(2)}) async-start(), calls=%async_computation.5 | async-start | bytes 3145728 | tf_op jit(solution)/shard_map/psum | solution.py:64
  112.1 3.5 copy-start.1
  118.9 1.8 slice-start
  216.2 34.4 %copy-start.2 = (s32[16]{0:T(128)S(1)}, s32[16]{0:T(128)}, u32[]{:S(2)}) copy-start(s32[16]{0:T(128)} %param.18) | copy-start | bytes 196
  216.2 34.4 %copy-start.3 = (s32[16]{0:T(128)S(1)}, s32[16]{0:T(128)}, u32[]{:S(2)}) copy-start(s32[16]{0:T(128)} %param.19) | copy-start | bytes 196
Sparse Core Ops, SparseCore 0:
  9.1 36.9 all-gather.3
  119.0 74.7 all-reduce.6
